TPU v7x, 32 devices: a whole 2x2x4 slice. The times are simulated.
32 devices in a mesh: groups: 2 (over x), hit: 8 (over z, y), query: 2 (over core).
Axes of the slice: x: 2, y: 2, z: 4, core: 2. Of those that a mesh axis runs over, the one named last changes fastest.
Arguments:
- hits: bfloat16 [16384, 512], P(('groups', 'hit', 'query')), parts along dimension 0, may hold values from -24 to 24
- order: int32 [32, 512], P(('groups', 'hit', 'query')), parts along dimension 0, may hold values from 0 to 511, each once within a row
- valid: int32 [16384], P(('groups', 'hit', 'query')), parts along dimension 0, may hold values 0 or 1
- reach: int32 [16384], P(('groups', 'hit', 'query')), parts along dimension 0, may hold values from 128 to 512, as said below
- enc_wq: bfloat16 [512, 512], replicated, may hold values from -3 to 3
- enc_wk: bfloat16 [512, 512], replicated, may hold values from -1 to 1
- enc_wv: bfloat16 [512, 512], replicated, may hold values from -0.25 to 0.25
- enc_wo: bfloat16 [512, 512], replicated, may hold values from -0.25 to 0.25
- enc_gain1: float32 [512], replicated, may hold values from 0.5 to 1.5
- ffn_up: bfloat16 [512, 2048], replicated, may hold values from -0.25 to 0.25
- ffn_down: bfloat16 [2048, 512], replicated, may hold values from -0.125 to 0.125
- enc_gain2: float32 [512], replicated, may hold values from 0.5 to 1.5
- object_queries: bfloat16 [512, 512], P(('groups', 'hit', 'query')), parts along dimension 0, may hold values from -48 to 48
- dec_wq: bfloat16 [512, 512], replicated, may hold values from -8 to 8
- dec_wk: bfloat16 [512, 512], replicated, may hold values from -0.25 to 0.25
- dec_wv: bfloat16 [512, 512], replicated, may hold values from -0.25 to 0.25
- dec_wo: bfloat16 [512, 512], replicated, may hold values from -0.25 to 0.25
- dec_gain: float32 [512], replicated, may hold values from 0.5 to 1.5
- out_proj: bfloat16 [512, 512], replicated, may hold values from -0.25 to 0.25
Outputs:
- encoded: bfloat16 [16384, 512], P(('groups', 'hit', 'query')), parts along dimension 0
- decoded: bfloat16 [512, 512], P(('groups', 'hit', 'query')), parts along dimension 0
There are 2 independent parts, one for each index of `groups`. A program takes and returns all parts, laid end to end along the dimension named above; an argument that names none is the same for every part. Nothing has to cross between parts.
Inputs may be any that keep to these rules, and one draw needn't show every extreme that they name: The first hit of every block of 512 arrival positions has reach 512.
All inputs are finite; a program needn't handle non-finite values. No bound on the sum of `valid` on one device may be relied on, other than what follows from the above.
Results may differ from a plain program's by a relative error of at most 0.035.
Values may be sent and summed in bfloat16 or wider, within the bound.
No kernel may reach another device: no remote copies, remote signals or barrier semaphores. Data moves between devices by JAX's collectives and lax.ppermute only.
A program may use at most 192 MiB of HBM per device.

v0:
```python
import math
import jax
import jax.numpy as jnp
from jax import lax
from jax.sharding import PartitionSpec as P

D = 512
HEADS = 8
WINDOW = 512


def padded(cells, sides, width):
    for axis, dim in sides:
        count = lax.axis_size(axis)
        head = lax.slice_in_dim(cells, 0, width, axis=dim)
        tail = lax.slice_in_dim(cells, cells.shape[dim] - width, cells.shape[dim], axis=dim)
        cells = jnp.concatenate(
            [
                lax.ppermute(tail, axis, [(i, (i + 1) % count) for i in range(count)]),
                cells,
                lax.ppermute(head, axis, [((i + 1) % count, i) for i in range(count)]),
            ],
            axis=dim,
        )
    return cells


def joined(value, axis, combine):
    everything = jax.tree.map(lambda part: lax.all_gather(part, axis), value)
    leading = jax.tree.map(lambda part: part[0], everything)

    def lap(k, so_far):
        return combine(so_far, jax.tree.map(lambda part: part[k], everything))

    return lax.fori_loop(1, lax.axis_size(axis), lap, leading)


def project(rows, weight):
    return jnp.dot(rows, weight, preferred_element_type=jnp.float32).astype(jnp.bfloat16)


def rms_norm(values, gain):
    scale = lax.rsqrt(jnp.mean(values * values, axis=-1, keepdims=True) + 1e-05)
    return values * scale * gain


def band_attention(queries, keys, values, key_valid, reach):
    count = queries.shape[0]
    span = keys.shape[0]
    margin = (span - count) // 2
    width = queries.shape[1] // HEADS
    query_heads = queries.reshape(count, HEADS, width)
    key_heads = keys.reshape(span, HEADS, width)
    value_heads = values.reshape(span, HEADS, width)
    scores = jnp.einsum(
        "qhd,khd->hqk", query_heads, key_heads, preferred_element_type=jnp.float32
    ) * (1.0 / math.sqrt(width))
    offset = jnp.arange(span, dtype=jnp.int32)[None, :] - (
        jnp.arange(count, dtype=jnp.int32)[:, None] + margin
    )
    allowed = (jnp.abs(offset) <= reach[:, None]) & ((key_valid[None, :] > 0) | (offset == 0))
    scores = jnp.where(allowed[None], scores, -jnp.inf)
    peak = jnp.max(scores, axis=2, keepdims=True)
    expo = jnp.where(allowed[None], jnp.exp(scores - peak), 0.0)
    probs = (expo / jnp.sum(expo, axis=2, keepdims=True)).astype(jnp.bfloat16)
    context = jnp.einsum("hqk,khd->qhd", probs, value_heads, preferred_element_type=jnp.float32)
    return context.reshape(count, HEADS * width).astype(jnp.bfloat16)


def encoder_tail(context, sorted_hits, enc_wo, enc_gain1, ffn_up, ffn_down, enc_gain2):
    attn_res = jnp.dot(context, enc_wo, preferred_element_type=jnp.float32) + sorted_hits.astype(
        jnp.float32
    )
    middle = rms_norm(attn_res, enc_gain1).astype(jnp.bfloat16)
    hidden = jax.nn.gelu(
        jnp.dot(middle, ffn_up, preferred_element_type=jnp.float32), approximate=True
    ).astype(jnp.bfloat16)
    ffn_res = jnp.dot(hidden, ffn_down, preferred_element_type=jnp.float32) + middle.astype(
        jnp.float32
    )
    return rms_norm(ffn_res, enc_gain2).astype(jnp.bfloat16)


def span_partial(queries, keys, values):
    count = queries.shape[0]
    span = keys.shape[0]
    width = queries.shape[1] // HEADS
    query_heads = queries.reshape(count, HEADS, width)
    key_heads = keys.reshape(span, HEADS, width)
    value_heads = values.reshape(span, HEADS, width)
    scores = jnp.einsum(
        "qhd,khd->qhk", query_heads, key_heads, preferred_element_type=jnp.float32
    ) * (1.0 / math.sqrt(width))
    peak = jnp.max(scores, axis=2)
    expo = jnp.exp(scores - peak[:, :, None])
    total = jnp.sum(expo, axis=2)
    weights = expo.astype(jnp.bfloat16)
    output = jnp.einsum("qhk,khd->qhd", weights, value_heads, preferred_element_type=jnp.float32)
    return (peak, total, output.reshape(count, HEADS * width))


def merge_partials(first, second):
    width = D // HEADS
    peak = jnp.maximum(first[0], second[0])
    left = jnp.exp(first[0] - peak)
    right = jnp.exp(second[0] - peak)
    total = first[1] * left + second[1] * right
    output = first[2] * jnp.repeat(left, width, axis=1) + second[2] * jnp.repeat(
        right, width, axis=1
    )
    return (peak, total, output)


def on_device(
    hits,
    order,
    valid,
    reach,
    enc_wq,
    enc_wk,
    enc_wv,
    enc_wo,
    enc_gain1,
    ffn_up,
    ffn_down,
    enc_gain2,
    object_queries,
    dec_wq,
    dec_wk,
    dec_wv,
    dec_wo,
    dec_gain,
    out_proj,
):
    rows = hits.shape[0]
    place = order[0]
    sorted_hits = hits[place]
    sorted_valid = valid[place].astype(jnp.bfloat16)
    sorted_reach = reach[place]
    queries = project(sorted_hits, enc_wq)
    wide_hits, wide_valid = (
        padded(sorted_hits, ((("hit", "query"), 0),), WINDOW),
        padded(sorted_valid, ((("hit", "query"), 0),), WINDOW),
    )
    wide_keys = project(wide_hits, enc_wk)
    wide_values = project(wide_hits, enc_wv)
    block = 512

    def attend(index):
        start = index * block
        return band_attention(queries, wide_keys, wide_values, wide_valid, sorted_reach)

    context = lax.map(attend, jnp.arange(rows // block, dtype=jnp.int32)).reshape(
        rows, queries.shape[1]
    )
    encoded = encoder_tail(context, sorted_hits, enc_wo, enc_gain1, ffn_up, ffn_down, enc_gain2)
    local_queries = project(object_queries, dec_wq)
    span_keys, span_values = (
        lax.all_gather(project(encoded, dec_wk), "query", axis=0, tiled=True),
        lax.all_gather(project(encoded, dec_wv), "query", axis=0, tiled=True),
    )
    all_queries = lax.all_gather(local_queries, "hit", axis=0, tiled=True)
    count = all_queries.shape[0]
    qblock = 512 if count % 512 == 0 else count

    def partial_block(index):
        return span_partial(all_queries, span_keys, span_values)

    peaks, totals, outputs = lax.map(partial_block, jnp.arange(count // qblock, dtype=jnp.int32))
    width = D // HEADS
    peaks = peaks.reshape(count, HEADS)
    totals = totals.reshape(count, HEADS)
    outputs = outputs.reshape(count, HEADS * width)
    owned = object_queries.shape[0]
    highest, merged_total, merged_out = joined((peaks, totals, outputs), "hit", merge_partials)
    start = lax.axis_index("hit") * owned
    numer = lax.dynamic_slice_in_dim(merged_out, start, owned, 0)
    denom = lax.dynamic_slice_in_dim(merged_total, start, owned, 0)
    cross = (numer / jnp.repeat(denom, width, axis=1)).astype(jnp.bfloat16)
    dec_res = jnp.dot(cross, dec_wo, preferred_element_type=jnp.float32) + object_queries.astype(
        jnp.float32
    )
    normed = rms_norm(dec_res, dec_gain).astype(jnp.bfloat16)
    decoded = jnp.dot(normed, out_proj, preferred_element_type=jnp.float32).astype(jnp.bfloat16)
    return (encoded, decoded)


def solution(mesh):
    in_specs = (
        P(("groups", "hit", "query"), None),
        P(("groups", "hit", "query"), None),
        P(("groups", "hit", "query")),
        P(("groups", "hit", "query")),
        P(),
        P(),
        P(),
        P(),
        P(),
        P(),
        P(),
        P(),
        P(("groups", "hit", "query"), None),
        P(),
        P(),
        P(),
        P(),
        P(),
        P(),
    )
    out_specs = (P(("groups", "hit", "query"), None), P(("groups", "hit", "query"), None))
    return jax.shard_map(
        on_device, mesh=mesh, in_specs=in_specs, out_specs=out_specs, check_vma=False
    )
```

profile of v0, /device:TPU:0, one launch (start us, length us, event | category | flops | bytes accessed | tf_op | source)
XLA Modules:
  0.0 208.7 jit_solution(11262240188574677869)
XLA Ops:
  8.1 3.1 %gather_fusion = bf16[512,512]{1,0:T(8,128)(2,1)S(1)} fusion(bf16[512,512]{1,0:T(8,128)(2,1)} %param.21, s32[1024]{0:T(1024)S(1)} %pad_clamp_fusion), kind=kCustom, calls=%fused_computation | custom fusion | bytes 1050624 | tf_op jit(solution)/shard_map/gather | solution.py:137
  11.7 5.0 %collective-permute-start.1 = (bf16[512,512]{1,0:T(8,128)(2,1)S(1)}, bf16[512,512]{1,0:T(8,128)(2,1)}, u32[]{:S(2)}, u32[]{:S(2)}) collective-permute-start(bf16[512,512]{1,0:T(8,128)(2,1)S(1)} %gather_fusion), channel_id=1, source_target_pairs={{1,0},{2,1},{3,2},{4,3},{5,4},{6,5},{7,6},{8,7},{9,8},{10,9},{11,1... | collective-permute-start | bytes 1572872 | tf_op jit(solution)/shard_map/ppermute | solution.py:21
  16.8 3.5 %gather_fusion.2 = s32[512]{0:T(512)S(1)} fusion(s32[512]{0:T(512)S(1)} %copy-done.1, s32[1024]{0:T(1024)S(1)} %pad_clamp_fusion), kind=kCustom, calls=%fused_computation.2 | custom fusion | bytes 6144 | tf_op jit(solution)/shard_map/gather | solution.py:138
  20.4 4.4 %collective-permute-start.3 = (bf16[512]{0:T(512)(128)(2,1)S(1)}, bf16[512]{0:T(512)(128)(2,1)S(1)}, u32[]{:S(2)}, u32[]{:S(2)}) collective-permute-start(bf16[512]{0:T(512)(128)(2,1)S(1)} %convert_element_type.70), channel_id=1, source_target_pairs={{1,0},{2,1},{3,2},{4,3},{5,4},{6,5},{7,6},{8,7},{9,8},{10,9},{11,1... | collective-permute-start | bytes 3080 | tf_op jit(solution)/shard_map/ppermute | solution.py:21
  24.8 2.3 %convolution_convert_fusion.4 = bf16[512,512]{0,1:T(8,128)(2,1)} fusion(bf16[512,512]{1,0:T(8,128)(2,1)S(1)} %gather_fusion, bf16[512,512]{1,0:T(8,128)(2,1)} %param.25), kind=kOutput, calls=%fused_computation.52 | convolution fusion | flops 268697600 | bytes 1572864 | tf_op jit(solution)/shard_map/dot_general | solution.py:39
  27.3 3.5 %gather_fusion.1 = s32[512]{0:T(512)S(1)} fusion(s32[512]{0:T(512)S(1)} %copy-done.2, s32[1024]{0:T(1024)S(1)} %pad_clamp_fusion), kind=kCustom, calls=%fused_computation.1 | custom fusion | bytes 6144 | tf_op jit(solution)/shard_map/gather | solution.py:139
  30.9 2.5 %fusion.21 = pred[512,1536]{1,0:T(8,128)(4,1)} fusion(s32[512]{0:T(512)S(1)} %gather_fusion.1, s32[512]{0:T(512)S(1)} %iota_add_fusion, pred[1536]{0:T(1024)(128)(4,1)S(1)} %maximum_compare_fusion), kind=kLoop, calls=%fused_computation.39 | loop fusion | flops 4718592 | bytes 792064 | tf_op jit(solution)/shard_map/while/body/eval_jaxpr/and | solution.py:61
  35.6 3.3 %convolution_convert_fusion = bf16[1536,512]{0,1:T(8,128)(2,1)} fusion(bf16[1536,512]{1,0:T(8,128)(2,1)S(1)} %constant_dynamic-update-slice_fusion, bf16[512,512]{1,0:T(8,128)(2,1)} %param.26), kind=kOutput, calls=%fused_computation.41 | convolution fusion | flops 806092800 | bytes 3670016 | tf_op jit(solution)/shard_map/dot_general | solution.py:39
  38.9 2.2 %convolution_convert_fusion.1 = bf16[1536,512]{0,1:T(8,128)(2,1)} fusion(bf16[1536,512]{1,0:T(8,128)(2,1)S(1)} %constant_dynamic-update-slice_fusion, bf16[512,512]{1,0:T(8,128)(2,1)S(1)} %copy-done.11), kind=kOutput, calls=%fused_computation.42 | convolution fusion | flops 806092800 | bytes 3670016 | tf_op jit(solution)/shard_map/dot_general | solution.py:39
  41.1 16.0 %fusion.47 = (f32[8,512]{1,0:T(8,128)S(1)}, f32[8,512,1536]{2,1,0:T(8,128)}) fusion(pred[512,1536]{1,0:T(8,128)(4,1)S(1)} %copy-done.4, bf16[512,8,64]{0,2,1:T(8,128)(2,1)} %bitcast.90, bf16[1536,8,64]{0,2,1:T(8,128)(2,1)} %bitcast.97), kind=kOutput, calls=%fused_computation.87 | convolution fusion | flops 836765184 | bytes 28065792 | tf_op jit(solution)/shard_map/while/body/eval_jaxpr/sub | solution.py:64
  57.1 11.0 %fusion.32 = bf16[8,64,512]{2,1,0:T(8,128)(2,1)S(1)} fusion(bf16[1536,8,64]{0,2,1:T(8,128)(2,1)} %bitcast.96, f32[8,512,1536]{2,1,0:T(8,128)} %get-tuple-element.255, f32[8,512]{1,0:T(8,128)S(1)} %get-tuple-element.254), kind=kOutput, calls=%fused_computation.49 | convolution fusion | flops 818151424 | bytes 27279360 | tf_op jit(solution)/shard_map/while/body/eval_jaxpr/hqk,khd->qhd/dot_general | solution.py:66
  69.6 6.4 %multiply_reduce_fusion = (f32[512]{0:T(512)S(1)}, f32[512,512]{0,1:T(8,128)}) fusion(f32[512]{0:T(512)S(1)} %copy-done.12, f32[512,512]{0,1:T(8,128)} %get-tuple-element.257, f32[512]{0:T(512)S(1)} %add_rsqrt_fusion.1, bf16[2048,512]{1,0:T(8,128)(2,1)S(1)} %copy-done, bf16[512,2048]{1,0:T(8,128)(2,1)} %param.30), kind=kOutput, calls=%fused_computation.57 | convolution fusion | flops 2159541760 | bytes 6297600 | tf_op jit(solution)/shard_map/dot_general | solution.py:78
  77.4 2.5 %convolution_convert_fusion.3 = bf16[512,512]{1,0:T(8,128)(2,1)} fusion(bf16[512,512]{0,1:T(8,128)(2,1)S(1)} %multiply_convert_fusion, bf16[512,512]{1,0:T(8,128)(2,1)} %param.35), kind=kOutput, calls=%fused_computation.51 | convolution fusion | flops 268697600 | bytes 1572864 | tf_op jit(solution)/shard_map/dot_general | solution.py:39
  80.0 2.4 %convolution_convert_fusion.2 = bf16[512,512]{1,0:T(8,128)(2,1)} fusion(bf16[512,512]{0,1:T(8,128)(2,1)S(1)} %multiply_convert_fusion, bf16[512,512]{1,0:T(8,128)(2,1)} %param.36), kind=kOutput, calls=%fused_computation.50 | convolution fusion | flops 268697600 | bytes 1572864 | tf_op jit(solution)/shard_map/dot_general | solution.py:39
  82.6 30.5 %all_gather.19 = bf16[128,512]{1,0:T(8,128)(2,1)S(1)} all-gather(bf16[16,512]{1,0:T(8,128)(2,1)S(1)} %convolution_convert_fusion.6), channel_id=1, replica_groups=mesh['groups'=2,'hit'=8,'query'=2] {'hit'}, dimensions={0}, use_global_device_ids=true | all-gather | bytes 147456 | tf_op jit(solution)/shard_map/all_gather | solution.py:162
  113.3 1.5 copy.38
  114.8 2.8 %bitcast_reduce_fusion = (f32[128,8]{0,1:T(8,128)S(1)}, f32[8,1024,128]{2,1,0:T(8,128)}) fusion(bf16[1024,8,64]{0,2,1:T(8,128)(2,1)S(1)} %bitcast.87, bf16[128,8,64]{0,2,1:T(8,128)(2,1)S(1)} %bitcast.91), kind=kOutput, calls=%fused_computation.32 | convolution fusion | flops 136313856 | bytes 5378048 | tf_op jit(solution)/shard_map/while/body/eval_jaxpr/qhd,khd->qhk/dot_general | solution.py:91
  119.1 3.0 %fusion.23 = f32[8,64,128]{2,1,0:T(8,128)S(1)} fusion(bf16[1024,8,64]{0,2,1:T(8,128)(2,1)S(1)} %bitcast.88, f32[8,1024,128]{2,1,0:T(8,128)} %get-tuple-element.261, f32[128,8]{0,1:T(8,128)S(1)} %get-tuple-element.260), kind=kOutput, calls=%fused_computation.43 | convolution fusion | flops 137363456 | bytes 5509120 | tf_op jit(solution)/shard_map/while/body/eval_jaxpr/qhk,khd->qhd/dot_general | solution.py:98
  123.0 2.0 copy.45
  125.1 2.9 %fusion.19 = f32[128,8]{0,1:T(8,128)S(1)} fusion(f32[8,1024,128]{2,1,0:T(8,128)} %get-tuple-element.261, f32[128,8]{0,1:T(8,128)S(1)} %get-tuple-element.260), kind=kLoop, calls=%fused_computation.35 | loop fusion | flops 3144704 | bytes 4202496 | tf_op jit(solution)/shard_map/while/body/eval_jaxpr/reduce_sum | solution.py:96
  127.9 31.0 %all-gather.1 = f32[1024,8]{0,1:T(8,128)S(1)} all-gather(f32[128,8]{0,1:T(8,128)S(1)} %fusion.19), channel_id=3, replica_groups=mesh['groups'=2,'hit'=8,'query'=2] {'hit'}, dimensions={0}, use_global_device_ids=true | all-gather | bytes 36864 | tf_op jit(solution)/shard_map/all_gather | solution.py:29
  159.0 30.8 %all-gather = f32[1024,8]{0,1:T(8,128)S(1)} all-gather(f32[128,8]{0,1:T(8,128)S(1)} %get-tuple-element.260), channel_id=2, replica_groups=mesh['groups'=2,'hit'=8,'query'=2] {'hit'}, dimensions={0}, use_global_device_ids=true | all-gather | bytes 36864 | tf_op jit(solution)/shard_map/all_gather | solution.py:29
  190.9 8.8 %while.12 = (s32[]{:T(128)}, f32[128,8]{0,1:T(8,128)S(1)}, f32[128,8]{0,1:T(8,128)S(1)}, f32[128,512]{0,1:T(8,128)S(1)}, f32[8,128,8]{1,2,0:T(8,128)S(1)}, /*ind...) while((s32[]{:T(128)}, f32[128,8]{0,1:T(8,128)S(1)}, ...), condition=%wide.region_7.8_spmd, body=%wide.region_6.7_spmd.sunk | while | flops 202757 | bytes 1876119 | solution.py:35
  200.3 1.9 convolution_convert_fusion.5
  (94 shorter events, 19.8 us)
Async XLA Ops:
  7.2 62.4 %copy-start = (bf16[2048,512]{1,0:T(8,128)(2,1)S(1)}, bf16[2048,512]{1,0:T(8,128)(2,1)}, u32[]{:S(2)}) copy-start(bf16[2048,512]{1,0:T(8,128)(2,1)} %param.31) | copy-start | bytes 6291460
  7.2 9.6 %copy-start.1 = (s32[512]{0:T(512)S(1)}, s32[512]{0:T(512)}, u32[]{:S(2)}) copy-start(s32[512]{0:T(512)} %param.23) | copy-start | bytes 6148
  7.2 106.1 %all-gather.6.cloned.1.call-start = ((), (), s32[]{:S(2)}) async-start(), calls=%async_computation | async-start | bytes 1572864 | tf_op jit(solution)/shard_map/all_gather | solution.py:159
  8.1 19.3 %copy-start.2 = (s32[512]{0:T(512)S(1)}, s32[512]{0:T(512)}, u32[]{:S(2)}) copy-start(s32[512]{0:T(512)} %param.24) | copy-start | bytes 6148
  11.2 22.2 %collective-permute-start = (bf16[512,512]{1,0:T(8,128)(2,1)S(1)}, bf16[512,512]{1,0:T(8,128)(2,1)}, u32[]{:S(2)}, u32[]{:S(2)}) collective-permute-start(bf16[512,512]{1,0:T(8,128)(2,1)S(1)} %gather_fusion), channel_id=1, source_target_pairs={{0,1},{1,2},{2,3},{3,4},{4,5},{5,6},{6,7},{7,8},{8,9},{9,10},{10,1... | collective-permute-start | bytes 1572872 | tf_op jit(solution)/shard_map/ppermute | solution.py:19
  11.7 22.8 %collective-permute-start.1 = (bf16[512,512]{1,0:T(8,128)(2,1)S(1)}, bf16[512,512]{1,0:T(8,128)(2,1)}, u32[]{:S(2)}, u32[]{:S(2)}) collective-permute-start(bf16[512,512]{1,0:T(8,128)(2,1)S(1)} %gather_fusion), channel_id=1, source_target_pairs={{1,0},{2,1},{3,2},{4,3},{5,4},{6,5},{7,6},{8,7},{9,8},{10,9},{11,1... | collective-permute-start | bytes 1572872 | tf_op jit(solution)/shard_map/ppermute | solution.py:21
  20.3 10.5 %collective-permute-start.2 = (bf16[512]{0:T(512)(128)(2,1)S(1)}, bf16[512]{0:T(512)(128)(2,1)S(1)}, u32[]{:S(2)}, u32[]{:S(2)}) collective-permute-start(bf16[512]{0:T(512)(128)(2,1)S(1)} %convert_element_type.70), channel_id=1, source_target_pairs={{0,1},{1,2},{2,3},{3,4},{4,5},{5,6},{6,7},{7,8},{8,9},{9,10},{10,1... | collective-permute-start | bytes 3080 | tf_op jit(solution)/shard_map/ppermute | solution.py:19
  20.4 10.5 %collective-permute-start.3 = (bf16[512]{0:T(512)(128)(2,1)S(1)}, bf16[512]{0:T(512)(128)(2,1)S(1)}, u32[]{:S(2)}, u32[]{:S(2)}) collective-permute-start(bf16[512]{0:T(512)(128)(2,1)S(1)} %convert_element_type.70), channel_id=1, source_target_pairs={{1,0},{2,1},{3,2},{4,3},{5,4},{6,5},{7,6},{8,7},{9,8},{10,9},{11,1... | collective-permute-start | bytes 3080 | tf_op jit(solution)/shard_map/ppermute | solution.py:21
  30.9 8.1 %copy-start.11 = (bf16[512,512]{1,0:T(8,128)(2,1)S(1)}, bf16[512,512]{1,0:T(8,128)(2,1)}, u32[]{:S(2)}) copy-start(bf16[512,512]{1,0:T(8,128)(2,1)} %param.27) | copy-start | bytes 1572868
  35.6 5.5 %copy-start.4 = (pred[512,1536]{1,0:T(8,128)(4,1)S(1)}, pred[512,1536]{1,0:T(8,128)(4,1)}, u32[]{:S(2)}) copy-start(pred[512,1536]{1,0:T(8,128)(4,1)} %fusion.21) | copy-start | bytes 2359300
  57.1 11.0 %copy-start.7 = (bf16[512,512]{1,0:T(8,128)(2,1)S(1)}, bf16[512,512]{1,0:T(8,128)(2,1)}, u32[]{:S(2)}) copy-start(bf16[512,512]{1,0:T(8,128)(2,1)} %param.28) | copy-start | bytes 1572868
  57.1 12.5 %copy-start.12 = (f32[512]{0:T(512)S(1)}, f32[512]{0:T(512)}, u32[]{:S(2)}) copy-start(f32[512]{0:T(512)} %param.29) | copy-start | bytes 6148
  69.6 6.4 %copy-start.9 = (f32[512]{0:T(512)S(1)}, f32[512]{0:T(512)}, u32[]{:S(2)}) copy-start(f32[512]{0:T(512)} %param.32) | copy-start | bytes 6148
  76.0 6.5 %copy-start.6 = (bf16[512,512]{1,0:T(8,128)(2,1)S(1)}, bf16[512,512]{1,0:T(8,128)(2,1)}, u32[]{:S(2)}) copy-start(bf16[512,512]{1,0:T(8,128)(2,1)} %param.34) | copy-start | bytes 1572868
  76.0 6.5 %copy-start.8 = (bf16[16,512]{1,0:T(8,128)(2,1)S(1)}, bf16[16,512]{1,0:T(8,128)(2,1)}, u32[]{:S(2)}) copy-start(bf16[16,512]{1,0:T(8,128)(2,1)} %param.33) | copy-start | bytes 49156
  77.4 35.9 %copy-start.3 = (bf16[512,512]{0,1:T(8,128)(2,1)}, bf16[512,512]{0,1:T(8,128)(2,1)S(1)}, u32[]{:S(2)}) copy-start(bf16[512,512]{0,1:T(8,128)(2,1)S(1)} %multiply_convert_fusion) | copy-start | bytes 1572868
  80.0 37.6 %all-gather.8.cloned.1.call-start = ((), (), s32[]{:S(2)}) async-start(), calls=%async_computation.1 | async-start | bytes 1572864 | tf_op jit(solution)/shard_map/all_gather | solution.py:160
  82.4 107.3 %all-gather.10.cloned.1.call-start = ((), (), s32[]{:S(2)}) async-start(), calls=%async_computation.2 | async-start | bytes 2359296 | tf_op jit(solution)/shard_map/all_gather | solution.py:29
  190.8 9.1 %copy-start.5 = (bf16[512,512]{1,0:T(8,128)(2,1)S(1)}, bf16[512,512]{1,0:T(8,128)(2,1)}, u32[]{:S(2)}) copy-start(bf16[512,512]{1,0:T(8,128)(2,1)} %param.37) | copy-start | bytes 1572868
  190.9 9.4 %copy-start.10 = (f32[512]{0:T(512)S(1)}, f32[512]{0:T(512)}, u32[]{:S(2)}) copy-start(f32[512]{0:T(512)} %param.38) | copy-start | bytes 6148
Sparse Core Ops, SparseCore 0:
  80.1 6.6 all-gather.5
  88.3 10.1 all-gather.7
  123.1 47.2 all-gather.9
where the time goes:
time: 210 us; the launch traced here: 209 us
  blocking collectives  92.3 us (44%)
  matrix products  55.6 us (26%)
  local copies, waits for them, and re-layouts  27.4 us (13%)
  between operations  14.1 us (7%)
  starting transfers between devices  10.2 us (5%)
  other arithmetic  8.66 us (4%)
    all_gather x2, blocking collectives, joined(): everything = jax.tree.map(lambda part: lax.all_gather(part, axis), value)  61.8 us
    all_gather x1, blocking collectives, on_device(): all_queries = lax.all_gather(local_queries, 'hit', axis=0, tiled=True)  30.5 us
    sub x1, matrix products, band_attention(): expo = jnp.where(allowed[None], jnp.exp(scores - peak), 0.0)  16 us
    dot_general x6, matrix products, project(): jnp.dot(rows, weight, preferred_element_type=jnp.float32)  12.8 us
    dot_general x1, matrix products, band_attention(): jnp.einsum('hqk,khd->qhd', probs, value_heads, preferred_element_type=jnp...  11 us
    ppermute x2, starting transfers between devices, padded(): lax.ppermute(head, axis, [((i + 1) % count, i) for i in range(count)])  9.48 us
    dynamic_slice x14, local copies, waits for them, and re-layouts, lap(): return combine(so_far, jax.tree.map(lambda part: part[k], everything))  7.72 us
    dot_general x1, matrix products, encoder_tail(): jnp.dot(hidden, ffn_down, preferred_element_type=jnp.float32)  6.36 us
  transfers between devices with their start and end apart: 7, of which 0 were waited for; matrix products, arithmetic and copies ran while one was open for 12% of the time, Pallas kernels for 0%

commit v1 on v0

--- a/solution.py
+++ b/solution.py
@@ -159,7 +159,10 @@
         lax.all_gather(project(encoded, dec_wk), "query", axis=0, tiled=True),
         lax.all_gather(project(encoded, dec_wv), "query", axis=0, tiled=True),
     )
-    all_queries = lax.all_gather(local_queries, "hit", axis=0, tiled=True)
+    peers = lax.axis_size("hit")
+    parts = jnp.stack([local_queries for _ in range(peers)])
+    parts = lax.all_to_all(parts, "hit", split_axis=0, concat_axis=0)
+    all_queries = jnp.concatenate(parts, axis=0)
     count = all_queries.shape[0]
     qblock = 512 if count % 512 == 0 else count
 

time: 210 us -> 191 us (0.910)
  blocking collectives: 92.3 us -> 72 us
    all_gather x1 -> x0, blocking collectives: 30.5 us -> none  [on_device(): all_queries = lax.all_gather(local_queries, 'hit', axis=0, tiled=True)]
    all_to_all x0 -> x1, blocking collectives: none -> 9.74 us  [on_device(): parts = lax.all_to_all(parts, 'hit', split_axis=0, concat_axis=0)]
  transfers between devices with their start and end apart: 7 -> 7, of which waited for: 0 -> 1; matrix products, arithmetic and copies ran while one was open for 12% -> 13% of each run, Pallas kernels for 0% -> 0%
where the time goes in v1:
time: 191 us; the launch traced here: 190 us
  blocking collectives  72 us (38%)
  matrix products  55.7 us (29%)
  local copies, waits for them, and re-layouts  27.5 us (14%)
  between operations  14.1 us (7%)
  starting transfers between devices  10.2 us (5%)
  other arithmetic  8.66 us (5%)
    all_gather x2, blocking collectives, joined(): everything = jax.tree.map(lambda part: lax.all_gather(part, axis), value)  62.3 us
    sub x1, matrix products, band_attention(): expo = jnp.where(allowed[None], jnp.exp(scores - peak), 0.0)  16 us
    dot_general x6, matrix products, project(): jnp.dot(rows, weight, preferred_element_type=jnp.float32)  12.8 us
    dot_general x1, matrix products, band_attention(): jnp.einsum('hqk,khd->qhd', probs, value_heads, preferred_element_type=jnp...  11 us
    all_to_all x1, blocking collectives, on_device(): parts = lax.all_to_all(parts, 'hit', split_axis=0, concat_axis=0)  9.74 us
    ppermute x2, starting transfers between devices, padded(): lax.ppermute(head, axis, [((i + 1) % count, i) for i in range(count)])  9.48 us
    dynamic_slice x14, local copies, waits for them, and re-layouts, lap(): return combine(so_far, jax.tree.map(lambda part: part[k], everything))  7.72 us
    dot_general x1, matrix products, encoder_tail(): jnp.dot(hidden, ffn_down, preferred_element_type=jnp.float32)  6.36 us
  transfers between devices with their start and end apart: 7, of which 1 were waited for; matrix products, arithmetic and copies ran while one was open for 13% of the time, Pallas kernels for 0%

profile of v1, /device:TPU:0, one launch (start us, length us, event | category | flops | bytes accessed | tf_op | source)
XLA Modules:
  0.0 190.1 jit_solution(2230931386898895571)
XLA Ops:
  8.1 3.1 %gather_fusion = bf16[512,512]{1,0:T(8,128)(2,1)S(1)} fusion(bf16[512,512]{1,0:T(8,128)(2,1)} %param.21, s32[1024]{0:T(1024)S(1)} %pad_clamp_fusion), kind=kCustom, calls=%fused_computation | custom fusion | bytes 1050624 | tf_op jit(solution)/shard_map/gather | solution.py:137
  11.7 5.0 %collective-permute-start.1 = (bf16[512,512]{1,0:T(8,128)(2,1)S(1)}, bf16[512,512]{1,0:T(8,128)(2,1)}, u32[]{:S(2)}, u32[]{:S(2)}) collective-permute-start(bf16[512,512]{1,0:T(8,128)(2,1)S(1)} %gather_fusion), channel_id=1, source_target_pairs={{1,0},{2,1},{3,2},{4,3},{5,4},{6,5},{7,6},{8,7},{9,8},{10,9},{11,1... | collective-permute-start | bytes 1572872 | tf_op jit(solution)/shard_map/ppermute | solution.py:21
  16.8 3.5 %gather_fusion.2 = s32[512]{0:T(512)S(1)} fusion(s32[512]{0:T(512)S(1)} %copy-done.1, s32[1024]{0:T(1024)S(1)} %pad_clamp_fusion), kind=kCustom, calls=%fused_computation.2 | custom fusion | bytes 6144 | tf_op jit(solution)/shard_map/gather | solution.py:138
  20.4 4.4 %collective-permute-start.3 = (bf16[512]{0:T(512)(128)(2,1)S(1)}, bf16[512]{0:T(512)(128)(2,1)S(1)}, u32[]{:S(2)}, u32[]{:S(2)}) collective-permute-start(bf16[512]{0:T(512)(128)(2,1)S(1)} %convert_element_type.70), channel_id=1, source_target_pairs={{1,0},{2,1},{3,2},{4,3},{5,4},{6,5},{7,6},{8,7},{9,8},{10,9},{11,1... | collective-permute-start | bytes 3080 | tf_op jit(solution)/shard_map/ppermute | solution.py:21
  24.8 2.3 %convolution_convert_fusion.4 = bf16[512,512]{0,1:T(8,128)(2,1)} fusion(bf16[512,512]{1,0:T(8,128)(2,1)S(1)} %gather_fusion, bf16[512,512]{1,0:T(8,128)(2,1)} %param.25), kind=kOutput, calls=%fused_computation.52 | convolution fusion | flops 268697600 | bytes 1572864 | tf_op jit(solution)/shard_map/dot_general | solution.py:39
  27.3 3.5 %gather_fusion.1 = s32[512]{0:T(512)S(1)} fusion(s32[512]{0:T(512)S(1)} %copy-done.2, s32[1024]{0:T(1024)S(1)} %pad_clamp_fusion), kind=kCustom, calls=%fused_computation.1 | custom fusion | bytes 6144 | tf_op jit(solution)/shard_map/gather | solution.py:139
  30.9 2.5 %fusion.21 = pred[512,1536]{1,0:T(8,128)(4,1)} fusion(s32[512]{0:T(512)S(1)} %gather_fusion.1, s32[512]{0:T(512)S(1)} %iota_add_fusion, pred[1536]{0:T(1024)(128)(4,1)S(1)} %maximum_compare_fusion), kind=kLoop, calls=%fused_computation.39 | loop fusion | flops 4718592 | bytes 792064 | tf_op jit(solution)/shard_map/while/body/eval_jaxpr/and | solution.py:61
  35.6 3.3 %convolution_convert_fusion = bf16[1536,512]{0,1:T(8,128)(2,1)} fusion(bf16[1536,512]{1,0:T(8,128)(2,1)S(1)} %constant_dynamic-update-slice_fusion, bf16[512,512]{1,0:T(8,128)(2,1)} %param.26), kind=kOutput, calls=%fused_computation.41 | convolution fusion | flops 806092800 | bytes 3670016 | tf_op jit(solution)/shard_map/dot_general | solution.py:39
  38.9 2.2 %convolution_convert_fusion.1 = bf16[1536,512]{0,1:T(8,128)(2,1)} fusion(bf16[1536,512]{1,0:T(8,128)(2,1)S(1)} %constant_dynamic-update-slice_fusion, bf16[512,512]{1,0:T(8,128)(2,1)S(1)} %copy-done.11), kind=kOutput, calls=%fused_computation.42 | convolution fusion | flops 806092800 | bytes 3670016 | tf_op jit(solution)/shard_map/dot_general | solution.py:39
  41.1 16.0 %fusion.49 = (f32[8,512]{1,0:T(8,128)S(1)}, f32[8,512,1536]{2,1,0:T(8,128)}) fusion(pred[512,1536]{1,0:T(8,128)(4,1)S(1)} %copy-done.4, bf16[512,8,64]{0,2,1:T(8,128)(2,1)} %bitcast.88, bf16[1536,8,64]{0,2,1:T(8,128)(2,1)} %bitcast.94), kind=kOutput, calls=%fused_computation.89 | convolution fusion | flops 836765184 | bytes 28065792 | tf_op jit(solution)/shard_map/while/body/eval_jaxpr/sub | solution.py:64
  57.1 11.0 %fusion.32 = bf16[8,64,512]{2,1,0:T(8,128)(2,1)S(1)} fusion(bf16[1536,8,64]{0,2,1:T(8,128)(2,1)} %bitcast.93, f32[8,512,1536]{2,1,0:T(8,128)} %get-tuple-element.255, f32[8,512]{1,0:T(8,128)S(1)} %get-tuple-element.254), kind=kOutput, calls=%fused_computation.49 | convolution fusion | flops 818151424 | bytes 27279360 | tf_op jit(solution)/shard_map/while/body/eval_jaxpr/hqk,khd->qhd/dot_general | solution.py:66
  69.6 6.4 %multiply_reduce_fusion = (f32[512]{0:T(512)S(1)}, f32[512,512]{0,1:T(8,128)}) fusion(f32[512]{0:T(512)S(1)} %copy-done.12, f32[512,512]{0,1:T(8,128)} %get-tuple-element.257, f32[512]{0:T(512)S(1)} %add_rsqrt_fusion.1, bf16[2048,512]{1,0:T(8,128)(2,1)S(1)} %copy-done, bf16[512,2048]{1,0:T(8,128)(2,1)} %param.30), kind=kOutput, calls=%fused_computation.57 | convolution fusion | flops 2159541760 | bytes 6297600 | tf_op jit(solution)/shard_map/dot_general | solution.py:78
  77.4 2.5 %convolution_convert_fusion.3 = bf16[512,512]{1,0:T(8,128)(2,1)} fusion(bf16[512,512]{0,1:T(8,128)(2,1)S(1)} %multiply_convert_fusion, bf16[512,512]{1,0:T(8,128)(2,1)} %param.35), kind=kOutput, calls=%fused_computation.51 | convolution fusion | flops 268697600 | bytes 1572864 | tf_op jit(solution)/shard_map/dot_general | solution.py:39
  80.0 2.4 %convolution_convert_fusion.2 = bf16[512,512]{1,0:T(8,128)(2,1)} fusion(bf16[512,512]{0,1:T(8,128)(2,1)S(1)} %multiply_convert_fusion, bf16[512,512]{1,0:T(8,128)(2,1)} %param.36), kind=kOutput, calls=%fused_computation.50 | convolution fusion | flops 268697600 | bytes 1572864 | tf_op jit(solution)/shard_map/dot_general | solution.py:39
  82.7 9.7 %all_to_all.5 = bf16[8,16,512]{2,1,0:T(8,128)(2,1)S(1)} all-to-all(bf16[8,16,512]{2,1,0:T(8,128)(2,1)S(1)} %stack.2), channel_id=1, replica_groups=mesh['groups'=2,'hit'=8,'query'=2] {'hit'}, dimensions={0} | all-to-all | bytes 262144 | tf_op jit(solution)/shard_map/all_to_all | solution.py:164
  94.1 2.8 %bitcast_reduce_fusion = (f32[128,8]{0,1:T(8,128)S(1)}, f32[8,1024,128]{2,1,0:T(8,128)}) fusion(bf16[1024,8,64]{0,2,1:T(8,128)(2,1)S(1)} %bitcast.85, bf16[128,8,64]{2,1,0:T(8,128)(2,1)S(1)} %reshape_reshape.4), kind=kOutput, calls=%fused_computation.32 | convolution fusion | flops 136313856 | bytes 5378048 | tf_op jit(solution)/shard_map/while/body/eval_jaxpr/qhd,khd->qhk/dot_general | solution.py:91
  96.9 1.6 all-gather.8.cloned.1.call-done
  100.1 3.0 %fusion.23 = f32[8,64,128]{2,1,0:T(8,128)S(1)} fusion(bf16[1024,8,64]{0,2,1:T(8,128)(2,1)S(1)} %bitcast.86, f32[8,1024,128]{2,1,0:T(8,128)} %get-tuple-element.261, f32[128,8]{0,1:T(8,128)S(1)} %get-tuple-element.260), kind=kOutput, calls=%fused_computation.43 | convolution fusion | flops 137363456 | bytes 5509120 | tf_op jit(solution)/shard_map/while/body/eval_jaxpr/qhk,khd->qhd/dot_general | solution.py:98
  104.0 2.0 %copy.45 = bf16[512,512]{1,0:T(8,128)(2,1)} copy(bf16[512,512]{0,1:T(8,128)(2,1)} %copy-done.3) | data formatting | bytes 1048576
  106.0 2.9 %fusion.19 = f32[128,8]{0,1:T(8,128)S(1)} fusion(f32[8,1024,128]{2,1,0:T(8,128)} %get-tuple-element.261, f32[128,8]{0,1:T(8,128)S(1)} %get-tuple-element.260), kind=kLoop, calls=%fused_computation.35 | loop fusion | flops 3144704 | bytes 4202496 | tf_op jit(solution)/shard_map/while/body/eval_jaxpr/reduce_sum | solution.py:96
  108.9 31.5 %all-gather.1 = f32[1024,8]{0,1:T(8,128)S(1)} all-gather(f32[128,8]{0,1:T(8,128)S(1)} %fusion.19), channel_id=3, replica_groups=mesh['groups'=2,'hit'=8,'query'=2] {'hit'}, dimensions={0}, use_global_device_ids=true | all-gather | bytes 36864 | tf_op jit(solution)/shard_map/all_gather | solution.py:29
  140.4 30.8 %all-gather = f32[1024,8]{0,1:T(8,128)S(1)} all-gather(f32[128,8]{0,1:T(8,128)S(1)} %get-tuple-element.260), channel_id=2, replica_groups=mesh['groups'=2,'hit'=8,'query'=2] {'hit'}, dimensions={0}, use_global_device_ids=true | all-gather | bytes 36864 | tf_op jit(solution)/shard_map/all_gather | solution.py:29
  172.3 8.8 %while.12 = (s32[]{:T(128)}, f32[128,8]{0,1:T(8,128)S(1)}, f32[128,8]{0,1:T(8,128)S(1)}, f32[128,512]{0,1:T(8,128)S(1)}, f32[8,128,8]{1,2,0:T(8,128)S(1)}, /*ind...) while((s32[]{:T(128)}, f32[128,8]{0,1:T(8,128)S(1)}, ...), condition=%wide.region_7.8_spmd, body=%wide.region_6.7_spmd.sunk | while | flops 202757 | bytes 1876119 | solution.py:35
  181.7 1.9 convolution_convert_fusion.5
  (95 shorter events, 21.4 us)
Async XLA Ops:
  7.2 62.4 %copy-start = (bf16[2048,512]{1,0:T(8,128)(2,1)S(1)}, bf16[2048,512]{1,0:T(8,128)(2,1)}, u32[]{:S(2)}) copy-start(bf16[2048,512]{1,0:T(8,128)(2,1)} %param.31) | copy-start | bytes 6291460
  7.2 9.6 %copy-start.1 = (s32[512]{0:T(512)S(1)}, s32[512]{0:T(512)}, u32[]{:S(2)}) copy-start(s32[512]{0:T(512)} %param.23) | copy-start | bytes 6148
  7.2 85.4 %all-gather.6.cloned.1.call-start = ((), (), s32[]{:S(2)}) async-start(), calls=%async_computation.1 | async-start | bytes 1572864 | tf_op jit(solution)/shard_map/all_gather | solution.py:159
  8.1 19.3 %copy-start.2 = (s32[512]{0:T(512)S(1)}, s32[512]{0:T(512)}, u32[]{:S(2)}) copy-start(s32[512]{0:T(512)} %param.24) | copy-start | bytes 6148
  11.2 22.2 %collective-permute-start = (bf16[512,512]{1,0:T(8,128)(2,1)S(1)}, bf16[512,512]{1,0:T(8,128)(2,1)}, u32[]{:S(2)}, u32[]{:S(2)}) collective-permute-start(bf16[512,512]{1,0:T(8,128)(2,1)S(1)} %gather_fusion), channel_id=1, source_target_pairs={{0,1},{1,2},{2,3},{3,4},{4,5},{5,6},{6,7},{7,8},{8,9},{9,10},{10,1... | collective-permute-start | bytes 1572872 | tf_op jit(solution)/shard_map/ppermute | solution.py:19
  11.7 22.8 %collective-permute-start.1 = (bf16[512,512]{1,0:T(8,128)(2,1)S(1)}, bf16[512,512]{1,0:T(8,128)(2,1)}, u32[]{:S(2)}, u32[]{:S(2)}) collective-permute-start(bf16[512,512]{1,0:T(8,128)(2,1)S(1)} %gather_fusion), channel_id=1, source_target_pairs={{1,0},{2,1},{3,2},{4,3},{5,4},{6,5},{7,6},{8,7},{9,8},{10,9},{11,1... | collective-permute-start | bytes 1572872 | tf_op jit(solution)/shard_map/ppermute | solution.py:21
  20.3 10.5 %collective-permute-start.2 = (bf16[512]{0:T(512)(128)(2,1)S(1)}, bf16[512]{0:T(512)(128)(2,1)S(1)}, u32[]{:S(2)}, u32[]{:S(2)}) collective-permute-start(bf16[512]{0:T(512)(128)(2,1)S(1)} %convert_element_type.70), channel_id=1, source_target_pairs={{0,1},{1,2},{2,3},{3,4},{4,5},{5,6},{6,7},{7,8},{8,9},{9,10},{10,1... | collective-permute-start | bytes 3080 | tf_op jit(solution)/shard_map/ppermute | solution.py:19
  20.4 10.5 %collective-permute-start.3 = (bf16[512]{0:T(512)(128)(2,1)S(1)}, bf16[512]{0:T(512)(128)(2,1)S(1)}, u32[]{:S(2)}, u32[]{:S(2)}) collective-permute-start(bf16[512]{0:T(512)(128)(2,1)S(1)} %convert_element_type.70), channel_id=1, source_target_pairs={{1,0},{2,1},{3,2},{4,3},{5,4},{6,5},{7,6},{8,7},{9,8},{10,9},{11,1... | collective-permute-start | bytes 3080 | tf_op jit(solution)/shard_map/ppermute | solution.py:21
  30.9 8.1 %copy-start.11 = (bf16[512,512]{1,0:T(8,128)(2,1)S(1)}, bf16[512,512]{1,0:T(8,128)(2,1)}, u32[]{:S(2)}) copy-start(bf16[512,512]{1,0:T(8,128)(2,1)} %param.27) | copy-start | bytes 1572868
  35.6 5.5 %copy-start.4 = (pred[512,1536]{1,0:T(8,128)(4,1)S(1)}, pred[512,1536]{1,0:T(8,128)(4,1)}, u32[]{:S(2)}) copy-start(pred[512,1536]{1,0:T(8,128)(4,1)} %fusion.21) | copy-start | bytes 2359300
  57.1 11.0 %copy-start.7 = (bf16[512,512]{1,0:T(8,128)(2,1)S(1)}, bf16[512,512]{1,0:T(8,128)(2,1)}, u32[]{:S(2)}) copy-start(bf16[512,512]{1,0:T(8,128)(2,1)} %param.28) | copy-start | bytes 1572868
  57.1 12.5 %copy-start.12 = (f32[512]{0:T(512)S(1)}, f32[512]{0:T(512)}, u32[]{:S(2)}) copy-start(f32[512]{0:T(512)} %param.29) | copy-start | bytes 6148
  69.6 6.4 %copy-start.9 = (f32[512]{0:T(512)S(1)}, f32[512]{0:T(512)}, u32[]{:S(2)}) copy-start(f32[512]{0:T(512)} %param.32) | copy-start | bytes 6148
  76.0 6.5 %copy-start.6 = (bf16[512,512]{1,0:T(8,128)(2,1)S(1)}, bf16[512,512]{1,0:T(8,128)(2,1)}, u32[]{:S(2)}) copy-start(bf16[512,512]{1,0:T(8,128)(2,1)} %param.34) | copy-start | bytes 1572868
  76.0 6.5 %copy-start.8 = (bf16[16,512]{1,0:T(8,128)(2,1)S(1)}, bf16[16,512]{1,0:T(8,128)(2,1)}, u32[]{:S(2)}) copy-start(bf16[16,512]{1,0:T(8,128)(2,1)} %param.33) | copy-start | bytes 49156
  77.4 15.2 %copy-start.3 = (bf16[512,512]{0,1:T(8,128)(2,1)}, bf16[512,512]{0,1:T(8,128)(2,1)S(1)}, u32[]{:S(2)}) copy-start(bf16[512,512]{0,1:T(8,128)(2,1)S(1)} %multiply_convert_fusion) | copy-start | bytes 1572868
  80.0 18.6 %all-gather.8.cloned.1.call-start = ((), (), s32[]{:S(2)}) async-start(), calls=%async_computation.2 | async-start | bytes 1572864 | tf_op jit(solution)/shard_map/all_gather | solution.py:160
  82.4 88.8 %all-gather.10.cloned.1.call-start = ((), (), s32[]{:S(2)}) async-start(), calls=%async_computation.3 | async-start | bytes 2359296 | tf_op jit(solution)/shard_map/all_gather | solution.py:29
  172.3 9.1 %copy-start.5 = (bf16[512,512]{1,0:T(8,128)(2,1)S(1)}, bf16[512,512]{1,0:T(8,128)(2,1)}, u32[]{:S(2)}) copy-start(bf16[512,512]{1,0:T(8,128)(2,1)} %param.37) | copy-start | bytes 1572868
  172.3 9.4 %copy-start.10 = (f32[512]{0:T(512)S(1)}, f32[512]{0:T(512)}, u32[]{:S(2)}) copy-start(f32[512]{0:T(512)} %param.38) | copy-start | bytes 6148
Sparse Core Ops, SparseCore 0:
  80.1 6.6 all-gather.5
  88.3 10.1 all-gather.7
  104.1 50.6 all-gather.9
